TPU v7x, 32 devices: a whole 2x2x4 slice. The times are simulated.
32 devices in a mesh: fsdp: 8 (over y, x, core), tp: 4 (over z).
Axes of the slice: x: 2, y: 2, z: 4, core: 2. Of those that a mesh axis runs over, the one named last changes fastest.
Arguments:
- features: bfloat16 [1024, 8192], P('fsdp'), may hold values from -17 to 17
- key_partials: bfloat16 [1024, 4, 128], P('fsdp', 'tp'), may hold values from -0.30935922 to 0.30935922
- momentum: float32 [4096, 4, 128], P('fsdp', 'tp'), may hold values from -6 to 6
Outputs:
- update: float32 [4096, 4, 128], P('fsdp', 'tp')
- new_momentum: float32 [4096, 4, 128], P('fsdp', 'tp')
All inputs are finite; a program needn't handle non-finite values.
Results may differ from a plain program's by a relative error of at most 0.0003.
Values may be sent and summed in bfloat16 or wider, within the bound.
No kernel may reach another device: no remote copies, remote signals or barrier semaphores. Data moves between devices by JAX's collectives and lax.ppermute only.
A program may use at most 64 MiB of HBM per device.

v0:
```python
import math
import jax
import jax.numpy as jnp
from jax import lax
from jax.sharding import PartitionSpec as P

D_W = 8192
ITERS = 5
retain = 0.95
first_coef = 3.4445
second_coef = -4.775
third_coef = 2.0315
epsilon = 1e-07
shrink = 0.2


def swapped(block, axis, distance):
    count = lax.axis_size(axis)
    route = []
    for low in range(count):
        high = low | 1 << distance
        if high != low and high < count:
            route += [(low, high), (high, low)]
    return lax.ppermute(block, axis, route)


def on_device(features, key_partials, momentum):
    precise = lax.Precision.HIGHEST
    contract = (((0,), (0,)), ((), ()))
    parity = lax.axis_index("tp") % 2
    own_part = key_partials[:, 0, :]
    head_size = key_partials.shape[2]
    rows_half = momentum.shape[0]
    shard = lax.psum_scatter(
        lax.dot_general(features, own_part, contract, preferred_element_type=jnp.float32),
        "fsdp",
        scatter_dimension=0,
        tiled=True,
    )
    pieces = shard.reshape(2, rows_half, head_size)
    mine = jnp.where(parity == 0, pieces[0], pieces[1])
    other = jnp.where(parity == 0, pieces[1], pieces[0])
    grads = mine + swapped(other, "tp", 0)
    moment = momentum[:, 0, :]
    fresh = retain * moment + grads
    blend = grads + retain * fresh
    gram = lax.dot_general(blend, blend, contract, precision=precise)
    gram = lax.psum(gram, "fsdp")
    gram = gram + swapped(gram, "tp", 0)
    inverse = 1.0 / (jnp.sqrt(jnp.trace(gram)) + epsilon)
    state = blend * inverse
    gram = gram * (inverse * inverse)
    identity = jnp.eye(head_size, dtype=jnp.float32)
    for step in range(ITERS):
        square = jnp.dot(gram, gram, precision=precise)
        poly = first_coef * identity + second_coef * gram + third_coef * square
        state = jnp.dot(state, poly, precision=precise)
        gram = jnp.dot(poly, jnp.dot(gram, poly, precision=precise), precision=precise)
    update = shrink * math.sqrt(D_W) * state
    return (update[:, None, :], fresh[:, None, :])


def solution(mesh):
    placed = (P("fsdp", None), P("fsdp", "tp", None), P("fsdp", "tp", None))
    return jax.shard_map(
        on_device,
        mesh=mesh,
        in_specs=placed,
        out_specs=(P("fsdp", "tp", None), P("fsdp", "tp", None)),
        check_vma=False,
    )
```

profile of v0, /device:TPU:0, one launch (start us, length us, event | category | flops | bytes accessed | tf_op | source)
XLA Modules:
  0.0 150.5 jit_solution(14905172062143592151)
XLA Ops:
  7.2 0.0 reduce-scatter.2.cloned.1.call-start
  7.2 1.5 %copy-done = bf16[128,8192]{1,0:T(8,128)(2,1)S(1)} copy-done((bf16[128,8192]{1,0:T(8,128)(2,1)S(1)}, bf16[128,8192]{1,0:T(8,128)(2,1)}, u32[]{:S(2)}) %copy-start) | copy-done | bytes 2097176
  8.8 3.4 %fusion.14 = f32[8192,128]{1,0:T(8,128)} fusion(bf16[128,8192]{1,0:T(8,128)(2,1)S(1)} %copy-done, bf16[128,1,128]{2,0,1:T(8,128)(2,1)} %param.4), kind=kOutput, calls=%fused_computation.29 | convolution fusion | flops 268435456 | bytes 6324224 | tf_op jit(solution)/shard_map/dot_general | solution.py:35
  12.2 0.0 all-reduce.2.cloned.1.call-start
  12.3 54.0 %reduce-scatter.2.cloned.1.call-done = f32[1024,128]{1,0:T(8,128)} async-done(((f32[8192,128]{1,0:T(8,128)}), f32[1024,128]{1,0:T(8,128)}) %reduce-scatter.2.cloned.1.call-update) | async-done | bytes 524304 | tf_op jit(solution)/shard_map/reduce_scatter | solution.py:34
  66.3 1.1 slice_select_fusion
  67.3 1.5 %collective-permute-start = (f32[512,128]{1,0:T(8,128)S(1)}, f32[512,128]{1,0:T(8,128)S(1)}, u32[]{:S(2)}, u32[]{:S(2)}) collective-permute-start(f32[512,128]{1,0:T(8,128)S(1)} %slice_select_fusion), channel_id=1, source_target_pairs={{0,1},{1,0},{2,3},{3,2},{4,5},{5,4},{6,7},{7,6},{8,9},{9,8},{10,11... | collective-permute-start | bytes 786440 | tf_op jit(solution)/shard_map/ppermute | solution.py:24
  68.9 6.4 %collective-permute-done = f32[512,128]{1,0:T(8,128)S(1)} collective-permute-done((f32[512,128]{1,0:T(8,128)S(1)}, f32[512,128]{1,0:T(8,128)S(1)}, u32[]{:S(2)}, u32[]{:S(2)}) %collective-permute-start) | collective-permute-done | bytes 262176 | tf_op jit(solution)/shard_map/ppermute | solution.py:24
  75.3 1.8 %bitcast_add_fusion = (f32[512,128]{1,0:T(8,128)}, f32[512,128]{1,0:T(8,128)S(1)}) fusion(f32[512,1,128]{2,0,1:T(8,128)S(1)} %bitcast.51, f32[512,128]{1,0:T(8,128)S(1)} %collective-permute-done, f32[1024,128]{1,0:T(8,128)} %reduce-scatter.2.cloned.1.call-done, pred[]{:T(512)S(6)} %eq.21), kind=kLoop, calls=%fused_computation.10 | loop fusion | flops 262144 | bytes 1572865 | tf_op jit(solution)/shard_map/add | solution.py:45
  77.1 1.2 fusion.7
  78.3 53.3 %all-reduce.2.cloned.1.call-done = f32[128,128]{1,0:T(8,128)} async-done(((f32[128,128]{1,0:T(8,128)}), f32[128,128]{1,0:T(8,128)}) %all-reduce.2.cloned.1.call-update) | async-done | bytes 65552 | tf_op jit(solution)/shard_map/psum | solution.py:48
  131.7 1.5 collective-permute-start.1
  133.2 3.0 %collective-permute-done.1 = f32[128,128]{1,0:T(8,128)S(1)} collective-permute-done((f32[128,128]{1,0:T(8,128)}, f32[128,128]{1,0:T(8,128)S(1)}, u32[]{:S(2)}, u32[]{:S(2)}) %collective-permute-start.1) | collective-permute-done | bytes 65568 | tf_op jit(solution)/shard_map/ppermute | solution.py:24
  136.2 1.5 select_reduce_fusion
  138.4 0.2 fusion.8
  138.6 0.4 fusion.4
  139.0 0.2 fusion.9
  139.2 0.2 fusion.20
  139.4 0.2 fusion.3
  139.6 0.2 fusion.22
  139.8 0.4 fusion.21
  140.2 0.2 fusion.23
  140.4 0.2 fusion.2
  140.6 0.2 fusion.25
  140.8 0.4 fusion.24
  141.2 0.2 fusion.26
  141.4 0.2 fusion.1
  141.6 0.2 fusion.28
  141.8 0.4 fusion.27
  142.2 0.2 fusion.29
  142.4 0.2 fusion
  142.6 1.1 convolution_multiply_fusion
  (5 shorter events, 0.0 us)
Async XLA Ops:
  7.2 1.6 %copy-start = (bf16[128,8192]{1,0:T(8,128)(2,1)S(1)}, bf16[128,8192]{1,0:T(8,128)(2,1)}, u32[]{:S(2)}) copy-start(bf16[128,8192]{1,0:T(8,128)(2,1)} %param.3) | copy-start | bytes 6291460
  7.2 59.1 %reduce-scatter.2.cloned.1.call-start = ((), (), s32[]{:S(2)}) async-start(), calls=%async_computation.1 | async-start | bytes 4718592 | tf_op jit(solution)/shard_map/reduce_scatter | solution.py:34
  12.2 63.1 %copy-start.1 = (f32[512,1,128]{2,1,0:T(1,128)S(1)}, f32[512,1,128]{2,1,0:T(1,128)}, u32[]{:S(2)}) copy-start(f32[512,1,128]{2,1,0:T(1,128)} %param.5) | copy-start | bytes 786436
  12.2 119.5 %all-reduce.2.cloned.1.call-start = ((), (), s32[]{:S(2)}) async-start(), calls=%async_computation.2 | async-start | bytes 131072 | tf_op jit(solution)/shard_map/psum | solution.py:48
  67.3 7.9 %collective-permute-start = (f32[512,128]{1,0:T(8,128)S(1)}, f32[512,128]{1,0:T(8,128)S(1)}, u32[]{:S(2)}, u32[]{:S(2)}) collective-permute-start(f32[512,128]{1,0:T(8,128)S(1)} %slice_select_fusion), channel_id=1, source_target_pairs={{0,1},{1,0},{2,3},{3,2},{4,5},{5,4},{6,7},{7,6},{8,9},{9,8},{10,11... | collective-permute-start | bytes 786440 | tf_op jit(solution)/shard_map/ppermute | solution.py:24
  131.7 4.5 %collective-permute-start.1 = (f32[128,128]{1,0:T(8,128)}, f32[128,128]{1,0:T(8,128)S(1)}, u32[]{:S(2)}, u32[]{:S(2)}) collective-permute-start(f32[128,128]{1,0:T(8,128)} %all-reduce.2.cloned.1.call-done), channel_id=1, source_target_pairs={{0,1},{1,0},{2,3},{3,2},{4,5},{5,4},{6,7},{7,6},{8,9},{9,8},{10,11... | collective-permute-start | bytes 196616 | tf_op jit(solution)/shard_map/ppermute | solution.py:24
Sparse Core Ops, SparseCore 0:
  12.4 53.8 reduce-scatter.1
  78.5 53.1 all-reduce.1
where the time goes:
time: 151 us
  waiting for transfers between devices  117 us (77%)
  between operations  14.9 us (10%)
  matrix products  9.86 us (7%)
  other arithmetic  4.35 us (3%)
  starting transfers between devices  3.11 us (2%)
  local copies, waits for them, and re-layouts  1.55 us (1%)
    reduce_scatter x1, waiting for transfers between devices, on_device(): lax.psum_scatter(lax.dot_general(features, own_part, contract, preferred_...  54 us
    psum x1, waiting for transfers between devices, on_device(): gram = lax.psum(gram, 'fsdp')  53.3 us
    ppermute x2, waiting for transfers between devices, swapped(): return lax.ppermute(block, axis, route)  9.37 us
    dot_general x1, matrix products, on_device(): lax.dot_general(features, own_part, contract, preferred_element_type=jnp....  3.45 us
    ppermute x2, starting transfers between devices, swapped(): return lax.ppermute(block, axis, route)  3.03 us
  transfers between devices with their start and end apart: 4, of which 4 were waited for; matrix products, arithmetic and copies ran while one was open for 0% of the time, Pallas kernels for 0%

commit v1 on v0

--- a/solution.py
+++ b/solution.py
@@ -45,7 +45,9 @@
     fresh = retain * moment + grads
     blend = grads + retain * fresh
     gram = lax.dot_general(blend, blend, contract, precision=precise)
-    gram = lax.psum(gram, "fsdp")
+    gram = gram
+    for hop in (1, 2, 4):
+        gram = gram + lax.ppermute(gram, "fsdp", [(dev, dev ^ hop) for dev in range(8)])
     gram = gram + swapped(gram, "tp", 0)
     inverse = 1.0 / (jnp.sqrt(jnp.trace(gram)) + epsilon)
     state = blend * inverse

time: 151 us -> 106 us (0.70)
  waiting for transfers between devices: 117 us -> 70 us
  starting transfers between devices: 3.11 us -> 6.29 us
    psum x1 -> x0, waiting for transfers between devices: 53.3 us -> none  [on_device(): gram = lax.psum(gram, 'fsdp')]
    ppermute x0 -> x3, waiting for transfers between devices: none -> 6.83 us  [on_device(): lax.ppermute(gram, 'fsdp', [(dev, dev ^ hop) for dev in range(8)])]
    ppermute x0 -> x3, starting transfers between devices: none -> 3.14 us  [on_device(): lax.ppermute(gram, 'fsdp', [(dev, dev ^ hop) for dev in range(8)])]
  transfers between devices with their start and end apart: 4 -> 6, of which waited for: 4 -> 6; matrix products, arithmetic and copies ran while one was open for 0% -> 0% of each run, Pallas kernels for 0% -> 0%
where the time goes in v1:
time: 106 us
  waiting for transfers between devices  70 us (66%)
  between operations  14.9 us (14%)
  matrix products  9.22 us (9%)
  starting transfers between devices  6.29 us (6%)
  other arithmetic  3.52 us (3%)
  local copies, waits for them, and re-layouts  1.55 us (1%)
    reduce_scatter x1, waiting for transfers between devices, on_device(): lax.psum_scatter(lax.dot_general(features, own_part, contract, preferred_...  54 us
    ppermute x2, waiting for transfers between devices, swapped(): return lax.ppermute(block, axis, route)  9.15 us
    ppermute x3, waiting for transfers between devices, on_device(): lax.ppermute(gram, 'fsdp', [(dev, dev ^ hop) for dev in range(8)])  6.83 us
    dot_general x1, matrix products, on_device(): lax.dot_general(features, own_part, contract, preferred_element_type=jnp....  3.45 us
    ppermute x3, starting transfers between devices, on_device(): lax.ppermute(gram, 'fsdp', [(dev, dev ^ hop) for dev in range(8)])  3.14 us
    ppermute x2, starting transfers between devices, swapped(): return lax.ppermute(block, axis, route)  3.11 us
    dot_general x5, matrix products, on_device(): state = jnp.dot(state, poly, precision=precise)  2.52 us
  transfers between devices with their start and end apart: 6, of which 6 were waited for; matrix products, arithmetic and copies ran while one was open for 0% of the time, Pallas kernels for 0%

profile of v1, /device:TPU:0, one launch (start us, length us, event | category | flops | bytes accessed | tf_op | source)
XLA Modules:
  0.0 105.5 jit_solution(10594878731344504261)
XLA Ops:
  7.2 1.5 %copy-done = bf16[128,8192]{1,0:T(8,128)(2,1)S(1)} copy-done((bf16[128,8192]{1,0:T(8,128)(2,1)S(1)}, bf16[128,8192]{1,0:T(8,128)(2,1)}, u32[]{:S(2)}) %copy-start) | copy-done | bytes 2097176
  8.8 3.5 %fusion.14 = f32[8192,128]{1,0:T(8,128)} fusion(bf16[128,8192]{1,0:T(8,128)(2,1)S(1)} %copy-done, bf16[128,1,128]{2,0,1:T(8,128)(2,1)} %param.4), kind=kOutput, calls=%fused_computation.29 | convolution fusion | flops 268435456 | bytes 6324224 | tf_op jit(solution)/shard_map/dot_general | solution.py:35
  12.3 54.0 %reduce-scatter.2.cloned.1.call-done = f32[1024,128]{1,0:T(8,128)} async-done(((f32[8192,128]{1,0:T(8,128)}), f32[1024,128]{1,0:T(8,128)}) %reduce-scatter.2.cloned.1.call-update) | async-done | bytes 524304 | tf_op jit(solution)/shard_map/reduce_scatter | solution.py:34
  66.3 1.1 %slice_select_fusion = f32[512,128]{1,0:T(8,128)S(1)} fusion(f32[1024,128]{1,0:T(8,128)} %reduce-scatter.2.cloned.1.call-done, pred[]{:T(512)S(6)} %eq.21), kind=kLoop, calls=%fused_computation.15 | loop fusion | flops 65536 | bytes 786433 | tf_op jit(solution)/shard_map/jit(_where)/select_n | solution.py:42
  67.3 1.5 %collective-permute-start = (f32[512,128]{1,0:T(8,128)S(1)}, f32[512,128]{1,0:T(8,128)S(1)}, u32[]{:S(2)}, u32[]{:S(2)}) collective-permute-start(f32[512,128]{1,0:T(8,128)S(1)} %slice_select_fusion), channel_id=1, source_target_pairs={{0,1},{1,0},{2,3},{3,2},{4,5},{5,4},{6,7},{7,6},{8,9},{9,8},{10,11... | collective-permute-start | bytes 786440 | tf_op jit(solution)/shard_map/ppermute | solution.py:24
  68.9 6.4 %collective-permute-done = f32[512,128]{1,0:T(8,128)S(1)} collective-permute-done((f32[512,128]{1,0:T(8,128)S(1)}, f32[512,128]{1,0:T(8,128)S(1)}, u32[]{:S(2)}, u32[]{:S(2)}) %collective-permute-start) | collective-permute-done | bytes 262176 | tf_op jit(solution)/shard_map/ppermute | solution.py:24
  75.3 1.8 %bitcast_add_fusion = (f32[512,128]{1,0:T(8,128)}, f32[512,128]{1,0:T(8,128)S(1)}) fusion(f32[512,1,128]{2,0,1:T(8,128)S(1)} %bitcast.51, f32[512,128]{1,0:T(8,128)S(1)} %collective-permute-done, f32[1024,128]{1,0:T(8,128)} %reduce-scatter.2.cloned.1.call-done, pred[]{:T(512)S(6)} %eq.21), kind=kLoop, calls=%fused_computation.10 | loop fusion | flops 262144 | bytes 1572865 | tf_op jit(solution)/shard_map/add | solution.py:45
  77.1 0.6 fusion.7
  77.8 1.2 %collective-permute-done.1 = f32[128,128]{1,0:T(8,128)S(1)} collective-permute-done((f32[128,128]{1,0:T(8,128)S(1)}, f32[128,128]{1,0:T(8,128)S(1)}, u32[]{:S(2)}, u32[]{:S(2)}) %collective-permute-start.1) | collective-permute-done | bytes 65568 | tf_op jit(solution)/shard_map/ppermute | solution.py:50
  79.0 1.5 %collective-permute-start.2 = (f32[128,128]{1,0:T(8,128)S(1)}, f32[128,128]{1,0:T(8,128)S(1)}, u32[]{:S(2)}, u32[]{:S(2)}) collective-permute-start(f32[128,128]{1,0:T(8,128)S(1)} %add.64), channel_id=1, source_target_pairs={{0,8},{4,12},{8,0},{12,4},{16,24},{20,28},{24,16},{28,20},{1,9},{5... | collective-permute-start | bytes 196616 | tf_op jit(solution)/shard_map/ppermute | solution.py:50
  80.6 2.8 %collective-permute-done.2 = f32[128,128]{1,0:T(8,128)S(1)} collective-permute-done((f32[128,128]{1,0:T(8,128)S(1)}, f32[128,128]{1,0:T(8,128)S(1)}, u32[]{:S(2)}, u32[]{:S(2)}) %collective-permute-start.2) | collective-permute-done | bytes 65568 | tf_op jit(solution)/shard_map/ppermute | solution.py:50
  83.4 1.5 %collective-permute-start.3 = (f32[128,128]{1,0:T(8,128)S(1)}, f32[128,128]{1,0:T(8,128)S(1)}, u32[]{:S(2)}, u32[]{:S(2)}) collective-permute-start(f32[128,128]{1,0:T(8,128)S(1)} %add.65), channel_id=1, source_target_pairs={{0,16},{4,20},{8,24},{12,28},{16,0},{20,4},{24,8},{28,12},{1,17},{... | collective-permute-start | bytes 196616 | tf_op jit(solution)/shard_map/ppermute | solution.py:50
  84.9 2.8 %collective-permute-done.3 = f32[128,128]{1,0:T(8,128)S(1)} collective-permute-done((f32[128,128]{1,0:T(8,128)S(1)}, f32[128,128]{1,0:T(8,128)S(1)}, u32[]{:S(2)}, u32[]{:S(2)}) %collective-permute-start.3) | collective-permute-done | bytes 65568 | tf_op jit(solution)/shard_map/ppermute | solution.py:50
  87.7 1.6 %collective-permute-start.4 = (f32[128,128]{1,0:T(8,128)S(1)}, f32[128,128]{1,0:T(8,128)S(1)}, u32[]{:S(2)}, u32[]{:S(2)}) collective-permute-start(f32[128,128]{1,0:T(8,128)S(1)} %add.66), channel_id=1, source_target_pairs={{0,1},{1,0},{2,3},{3,2},{4,5},{5,4},{6,7},{7,6},{8,9},{9,8},{10,11... | collective-permute-start | bytes 196616 | tf_op jit(solution)/shard_map/ppermute | solution.py:24
  89.3 2.8 %collective-permute-done.4 = f32[128,128]{1,0:T(8,128)S(1)} collective-permute-done((f32[128,128]{1,0:T(8,128)S(1)}, f32[128,128]{1,0:T(8,128)S(1)}, u32[]{:S(2)}, u32[]{:S(2)}) %collective-permute-start.4) | collective-permute-done | bytes 65568 | tf_op jit(solution)/shard_map/ppermute | solution.py:24
  92.0 0.6 select_reduce_fusion
  93.4 0.2 fusion.8
  93.6 0.4 fusion.4
  94.0 0.2 fusion.9
  94.2 0.2 fusion.20
  94.4 0.2 fusion.3
  94.8 0.4 fusion.21
  95.2 0.2 fusion.23
  95.4 0.2 fusion.2
  95.6 0.2 fusion.25
  95.8 0.4 fusion.24
  96.2 0.2 fusion.26
  96.4 0.2 fusion.1
  96.8 0.4 fusion.27
  97.2 0.2 fusion.29
  97.4 0.2 fusion
  97.6 1.1 %convolution_multiply_fusion = f32[512,128]{1,0:T(8,128)} fusion(f32[512,128]{1,0:T(8,128)S(1)} %fusion.27, f32[128,128]{1,0:T(8,128)S(1)} %fusion), kind=kOutput, calls=%fused_computation | convolution fusion | flops 100728832 | bytes 589824 | tf_op jit(solution)/shard_map/dot_general | solution.py:59
  (11 shorter events, 0.6 us)
Async XLA Ops:
  7.2 1.6 %copy-start = (bf16[128,8192]{1,0:T(8,128)(2,1)S(1)}, bf16[128,8192]{1,0:T(8,128)(2,1)}, u32[]{:S(2)}) copy-start(bf16[128,8192]{1,0:T(8,128)(2,1)} %param.3) | copy-start | bytes 6291460
  7.2 59.1 %reduce-scatter.2.cloned.1.call-start = ((), (), s32[]{:S(2)}) async-start(), calls=%async_computation.1 | async-start | bytes 4718592 | tf_op jit(solution)/shard_map/reduce_scatter | solution.py:34
  12.2 63.1 %copy-start.1 = (f32[512,1,128]{2,1,0:T(1,128)S(1)}, f32[512,1,128]{2,1,0:T(1,128)}, u32[]{:S(2)}) copy-start(f32[512,1,128]{2,1,0:T(1,128)} %param.5) | copy-start | bytes 786436
  67.3 7.9 %collective-permute-start = (f32[512,128]{1,0:T(8,128)S(1)}, f32[512,128]{1,0:T(8,128)S(1)}, u32[]{:S(2)}, u32[]{:S(2)}) collective-permute-start(f32[512,128]{1,0:T(8,128)S(1)} %slice_select_fusion), channel_id=1, source_target_pairs={{0,1},{1,0},{2,3},{3,2},{4,5},{5,4},{6,7},{7,6},{8,9},{9,8},{10,11... | collective-permute-start | bytes 786440 | tf_op jit(solution)/shard_map/ppermute | solution.py:24
  77.7 1.3 %collective-permute-start.1 = (f32[128,128]{1,0:T(8,128)S(1)}, f32[128,128]{1,0:T(8,128)S(1)}, u32[]{:S(2)}, u32[]{:S(2)}) collective-permute-start(f32[128,128]{1,0:T(8,128)S(1)} %fusion.7), channel_id=1, source_target_pairs={{0,4},{4,0},{8,12},{12,8},{16,20},{20,16},{24,28},{28,24},{1,5},{5... | collective-permute-start | bytes 196616 | tf_op jit(solution)/shard_map/ppermute | solution.py:50
  79.0 4.3 %collective-permute-start.2 = (f32[128,128]{1,0:T(8,128)S(1)}, f32[128,128]{1,0:T(8,128)S(1)}, u32[]{:S(2)}, u32[]{:S(2)}) collective-permute-start(f32[128,128]{1,0:T(8,128)S(1)} %add.64), channel_id=1, source_target_pairs={{0,8},{4,12},{8,0},{12,4},{16,24},{20,28},{24,16},{28,20},{1,9},{5... | collective-permute-start | bytes 196616 | tf_op jit(solution)/shard_map/ppermute | solution.py:50
  83.4 4.3 %collective-permute-start.3 = (f32[128,128]{1,0:T(8,128)S(1)}, f32[128,128]{1,0:T(8,128)S(1)}, u32[]{:S(2)}, u32[]{:S(2)}) collective-permute-start(f32[128,128]{1,0:T(8,128)S(1)} %add.65), channel_id=1, source_target_pairs={{0,16},{4,20},{8,24},{12,28},{16,0},{20,4},{24,8},{28,12},{1,17},{... | collective-permute-start | bytes 196616 | tf_op jit(solution)/shard_map/ppermute | solution.py:50
  87.7 4.3 %collective-permute-start.4 = (f32[128,128]{1,0:T(8,128)S(1)}, f32[128,128]{1,0:T(8,128)S(1)}, u32[]{:S(2)}, u32[]{:S(2)}) collective-permute-start(f32[128,128]{1,0:T(8,128)S(1)} %add.66), channel_id=1, source_target_pairs={{0,1},{1,0},{2,3},{3,2},{4,5},{5,4},{6,7},{7,6},{8,9},{9,8},{10,11... | collective-permute-start | bytes 196616 | tf_op jit(solution)/shard_map/ppermute | solution.py:24
Sparse Core Ops, SparseCore 0:
  12.4 53.8 reduce-scatter.1
